TPU v7x, 32 devices: a whole 2x2x4 slice. The times are simulated.
32 devices in a mesh: tm: 16 (over z, y, core), series: 2 (over x).
Axes of the slice: x: 2, y: 2, z: 4, core: 2. Of those that a mesh axis runs over, the one named last changes fastest.
Arguments:
- panel: bfloat16 [4096, 16384], P('series', 'tm'), may hold values from -6 to 6
- series_factors: bfloat16 [4096, 128], P('series'), may hold values from -1.796875 to 1.796875
- time_factors: bfloat16 [16384, 128], P('tm'), may hold values from -1.796875 to 1.796875
- ar_weights: float32 [16, 128], replicated, may hold values from -1 to 1
- tile_mask: int32 [32, 128], P('series', 'tm'), may hold values 0 or 1
- lags: int32 [16], replicated, may hold values from 1 to 128, as said below
Outputs:
- series_grad: float32 [4096, 128], P(('series', 'tm'))
- time_grad: float32 [16384, 128], P(('tm', 'series'))
- ar_grad: float32 [16, 128], replicated
Inputs may be any that keep to these rules, and one draw needn't show every extreme that they name: `lags`: strictly increasing, and the last equals 128.
All inputs are finite; a program needn't handle non-finite values. No bound on the sum of `tile_mask` on one device may be relied on, other than what follows from the above.
Results may differ from a plain program's by a relative error of at most 0.00045.
Values may be sent and summed in bfloat16 or wider, within the bound.
A program may use at most 64 MiB of HBM per device.

v0:
```python
import math
import jax
import jax.numpy as jnp
from jax import lax
from jax.sharding import PartitionSpec as P

NLAG = 16
LAGMAX = 128
TILE = 128
ar_strength = 1.0


def from_behind(value, axis, steps):
    count = lax.axis_size(axis)
    initial, last = (max(0, -steps), min(count, count - steps))
    return lax.ppermute(value, axis, [(source, source + steps) for source in range(initial, last)])


def lag_error(extended, weights, lags, count):
    total = extended[LAGMAX : LAGMAX + count]
    for lag_pos in range(NLAG):
        shifted = lax.dynamic_slice_in_dim(extended, LAGMAX - lags[lag_pos], count, 0)
        total = total - weights[lag_pos] * shifted
    return total


def per_device(panel, series_factors, time_factors, ar_weights, tile_mask, lags):
    time_rows = time_factors.shape[0]
    series_rows = series_factors.shape[0]
    time_devices = lax.axis_size("tm")
    series_devices = lax.axis_size("series")
    scale_time = 1.0 / math.sqrt(time_rows * time_devices)
    scale_series = 1.0 / math.sqrt(series_rows * series_devices)
    tm_index = lax.axis_index("tm")
    earlier = from_behind(time_factors[time_rows - LAGMAX :], "tm", 1)
    keep = jnp.repeat(jnp.repeat(tile_mask, TILE, 0), TILE, 1) > 0
    predicted = jnp.dot(series_factors, time_factors.T, preferred_element_type=jnp.float32)
    residual = jnp.where(keep, predicted - panel.astype(jnp.float32), jnp.float32(0.0)).astype(
        jnp.bfloat16
    )
    series_part = jnp.dot(residual, time_factors, preferred_element_type=jnp.float32) * scale_time
    time_part = (
        lax.dot_general(
            residual, series_factors, (((0,), (0,)), ((), ())), preferred_element_type=jnp.float32
        )
        * scale_series
    )
    factors32 = time_factors.astype(jnp.float32)
    extended = jnp.concatenate([earlier.astype(jnp.float32), factors32], axis=0)
    moments = tm_index * time_rows + jnp.arange(time_rows, dtype=jnp.int32)
    error = jnp.where(
        (moments >= LAGMAX)[:, None],
        lag_error(extended, ar_weights, lags, time_rows),
        jnp.float32(0.0),
    )
    upcoming = from_behind(error[:LAGMAX].astype(jnp.bfloat16), "tm", -1).astype(jnp.float32)
    error_ext = jnp.concatenate([error, upcoming], axis=0)
    adjoint = error
    ar_rows = []
    for lag_pos in range(NLAG):
        ahead = lax.dynamic_slice_in_dim(error_ext, lags[lag_pos], time_rows, 0)
        adjoint = adjoint - ar_weights[lag_pos] * ahead
        behind = lax.dynamic_slice_in_dim(extended, LAGMAX - lags[lag_pos], time_rows, 0)
        ar_rows.append(-scale_time * jnp.sum(error * behind, axis=0))
    ar_part = jnp.stack(ar_rows)
    series_grad = lax.psum_scatter(series_part, "tm", scatter_dimension=0, tiled=True)
    ar_grad = lax.psum(ar_part, "tm")
    time_share = lax.psum_scatter(time_part, "series", scatter_dimension=0, tiled=True)
    own_time = time_rows // series_devices
    adjoint_rows = lax.dynamic_slice_in_dim(
        adjoint, lax.axis_index("series") * own_time, own_time, 0
    )
    time_grad = time_share + ar_strength * adjoint_rows
    return (series_grad, time_grad, ar_grad)


def solution(mesh):
    in_specs = (P("series", "tm"), P("series", None), P("tm", None), P(), P("series", "tm"), P())
    out_specs = (P(("series", "tm"), None), P(("tm", "series"), None), P())
    return jax.shard_map(
        per_device, mesh=mesh, in_specs=in_specs, out_specs=out_specs, check_vma=False
    )
```

profile of v0, /device:TPU:0, one launch (start us, length us, event | category | flops | bytes accessed | tf_op | source)
XLA Modules:
  0.0 137.6 jit_solution(11205370588736498086)
XLA Ops:
  7.2 0.0 reduce-scatter.5.cloned.1.call-start
  7.2 0.7 broadcast_compare_fusion
  8.0 0.1 copy.9
  8.1 0.1 broadcast_in_dim.23
  8.1 6.4 %broadcast_in_dim.24 = pred[2048,8,128]{2,1,0:T(8,128)(4,1)S(1)} broadcast(pred[2048,8]{1,0:T(8,128)(4,1)S(1)} %bitcast.91), dimensions={0,1} | broadcast | bytes 2113536 | tf_op jit(solution)/shard_map/broadcast_in_dim | solution.py:36
  14.5 4.1 %select_convert_fusion = bf16[2048,1024]{1,0:T(8,128)(2,1)S(1)} fusion(bf16[2048,1024]{1,0:T(8,128)(2,1)} %param.6, pred[256,8,8,128]{3,2,1,0:T(8,128)(4,1)S(1)} %bitcast.90, bf16[2048,128]{1,0:T(8,128)(2,1)S(1)} %copy-done, bf16[1024,128]{1,0:T(8,128)(2,1)} %param.8), kind=kOutput, calls=%fused_computation | convolution fusion | flops 545259520 | bytes 11272192 | tf_op jit(solution)/shard_map/dot_general | solution.py:37
  18.6 1.9 %copy-done.1 = bf16[2048,1024]{1,0:T(8,128)(2,1)} copy-done((bf16[2048,1024]{1,0:T(8,128)(2,1)}, bf16[2048,1024]{1,0:T(8,128)(2,1)S(1)}, u32[]{:S(2)}) %copy-start.1) | copy-done | bytes 4194328
  20.5 2.1 %convolution_multiply_fusion.1 = f32[1024,128]{1,0:T(8,128)} fusion(bf16[2048,1024]{1,0:T(8,128)(2,1)S(1)} %select_convert_fusion, bf16[2048,128]{1,0:T(8,128)(2,1)S(1)} %copy-done), kind=kOutput, calls=%fused_computation.34 | convolution fusion | flops 537001984 | bytes 5242880 | tf_op jit(solution)/shard_map/dot_general | solution.py:43
  22.6 0.0 reduce-scatter.5.cloned.1.call-update
  22.6 0.0 reduce-scatter.3.cloned.1.call-start
  22.7 2.4 %collective-permute-start = (bf16[128,128]{1,0:T(8,128)(2,1)S(1)}, bf16[128,128]{1,0:T(8,128)(2,1)S(1)}, u32[]{:S(2)}, u32[]{:S(2)}) collective-permute-start(bf16[128,128]{1,0:T(8,128)(2,1)S(1)} %slice.70), channel_id=1, source_target_pairs={{0,2},{2,4},{4,6},{6,8},{8,10},{10,12},{12,14},{14,16},{16,18},{18... | collective-permute-start | bytes 98312 | tf_op jit(solution)/shard_map/ppermute | solution.py:16
  25.1 4.4 %convolution_multiply_fusion = f32[2048,128]{1,0:T(8,128)} fusion(bf16[2048,1024]{1,0:T(8,128)(2,1)} %copy-done.1, bf16[1024,128]{1,0:T(8,128)(2,1)S(1)} %copy-done.2), kind=kOutput, calls=%fused_computation.33 | convolution fusion | flops 537133056 | bytes 5505024 | tf_op jit(solution)/shard_map/dot_general | solution.py:41
  29.5 0.0 reduce-scatter.3.cloned.1.call-update
  29.6 0.7 fusion.63
  80.7 4.1 %multiply_reduce_fusion = (f32[128]{0:T(128)S(1)}, f32[128]{0:T(128)S(1)}, f32[128]{0:T(128)S(1)}, f32[128]{0:T(128)S(1)}, f32[128]{0:T(128)S(1)}, /*index=5*/f32[128]{0:T(128)S(1)}, f32[1024,128]{1,0:T(8,128)S(1)}) fusion(s32[]{:T(128)S(6)} %select_n.139, f32[1024,128]{1,0:T(8,128)S(1)} %convert_element_type.18, f32[128,128]{1,0:T(8,128)S(1)} %convert_element_type.19, ...), kind=kLoop, calls=%fused_computation.116 | loop fusion | flops 8912128 | bytes 1388608 | tf_op jit(solution)/shard_map/reduce_sum | solution.py:64
  84.8 0.5 multiply_reduce_fusion.12
  85.3 0.7 multiply_reduce_fusion.6
  86.0 1.3 collective-permute-start.1
  87.4 0.1 stack.2
  87.5 37.2 %psum.7 = f32[16,128]{1,0:T(8,128)} all-reduce(f32[16,128]{1,0:T(8,128)S(1)} %stack.2), channel_id=1, replica_groups=mesh['tm'=16,'series'=2] {'tm'}, use_global_device_ids=true, to_apply=%region_18.19 | all-reduce | flops 2048 | bytes 16384 | tf_op jit(solution)/shard_map/psum | solution.py:67
  124.6 0.5 fusion.31
  125.2 3.3 %fusion.11 = f32[1024,128]{1,0:T(8,128)S(1)} fusion(f32[1024,128]{1,0:T(8,128)S(1)} %get-tuple-element.19, s32[]{:T(128)S(6)} %select_n.141, s32[]{:T(128)S(6)} %select_n.142, s32[]{:T(128)S(6)} %select_n.143, s32[]{:T(128)S(6)} %select_n.144, s32[]{:T(128)S(6)} %select_n.145, s32[]{:T(128)S(6)} %select_n.146, s32[]{:T(128)S(6)} %select_n.147, ...), kind=kLoop, calls=%fused_computation.78 | loop fusion | flops 3932160 | bytes 1119272 | tf_op jit(solution)/shard_map/sub | solution.py:62
  128.4 0.0 reduce-scatter.5.cloned.1.call-done
  128.5 2.2 %fusion.52 = f32[512,128]{1,0:T(8,128)} fusion(f32[512,128]{1,0:T(8,128)} %reduce-scatter.5.cloned.1.call-done, s32[]{:T(128)S(6)} %add.192, f32[1024,128]{1,0:T(8,128)S(1)} %get-tuple-element.19, s32[]{:T(128)S(6)} %add.186, s32[]{:T(128)S(6)} %add.188, s32[]{:T(128)S(6)} %add.190, f32[128,128]{1,0:T(8,128)S(1)} %convert_element_type.20, ...), kind=kLoop, calls=%fused_computation.136 | loop fusion | flops 1048576 | bytes 1903124 | tf_op jit(solution)/shard_map/add | solution.py:73
  (27 shorter events, 0.1 us)
Async XLA Ops:
  7.2 7.3 %copy-start = (bf16[2048,128]{1,0:T(8,128)(2,1)S(1)}, bf16[2048,128]{1,0:T(8,128)(2,1)}, u32[]{:S(2)}) copy-start(bf16[2048,128]{1,0:T(8,128)(2,1)} %param.7) | copy-start | bytes 1572868
  7.2 121.3 %reduce-scatter.5.cloned.1.call-start = ((), (), s32[]{:S(2)}) async-start(), calls=%async_computation.3 | async-start | bytes 786432 | tf_op jit(solution)/shard_map/reduce_scatter | solution.py:68
  18.6 1.9 %copy-start.1 = (bf16[2048,1024]{1,0:T(8,128)(2,1)}, bf16[2048,1024]{1,0:T(8,128)(2,1)S(1)}, u32[]{:S(2)}) copy-start(bf16[2048,1024]{1,0:T(8,128)(2,1)S(1)} %select_convert_fusion) | copy-start | bytes 12582916
  20.5 2.2 %copy-start.2 = (bf16[1024,128]{1,0:T(8,128)(2,1)S(1)}, bf16[1024,128]{1,0:T(8,128)(2,1)}, u32[]{:S(2)}) copy-start(bf16[1024,128]{1,0:T(8,128)(2,1)} %param.8) | copy-start | bytes 786436
  22.6 7.0 %copy-start.3 = (s32[16]{0:T(128)S(1)}, s32[16]{0:T(128)}, u32[]{:S(2)}) copy-start(s32[16]{0:T(128)} %param.11) | copy-start | bytes 196
  22.6 7.7 %copy-start.4 = (f32[16,128]{1,0:T(8,128)S(1)}, f32[16,128]{1,0:T(8,128)}, u32[]{:S(2)}) copy-start(f32[16,128]{1,0:T(8,128)} %param.9) | copy-start | bytes 24580
  22.6 108.1 %reduce-scatter.3.cloned.1.call-start = ((), (), s32[]{:S(2)}) async-start(), calls=%async_computation.2 | async-start | bytes 1114112 | tf_op jit(solution)/shard_map/reduce_scatter | solution.py:66
  22.7 58.0 %collective-permute-start = (bf16[128,128]{1,0:T(8,128)(2,1)S(1)}, bf16[128,128]{1,0:T(8,128)(2,1)S(1)}, u32[]{:S(2)}, u32[]{:S(2)}) collective-permute-start(bf16[128,128]{1,0:T(8,128)(2,1)S(1)} %slice.70), channel_id=1, source_target_pairs={{0,2},{2,4},{4,6},{6,8},{8,10},{10,12},{12,14},{14,16},{16,18},{18... | collective-permute-start | bytes 98312 | tf_op jit(solution)/shard_map/ppermute | solution.py:16
  86.0 38.6 %collective-permute-start.1 = (bf16[128,128]{1,0:T(8,128)(2,1)S(1)}, bf16[128,128]{1,0:T(8,128)(2,1)S(1)}, u32[]{:S(2)}, u32[]{:S(2)}) collective-permute-start(bf16[128,128]{1,0:T(8,128)(2,1)S(1)} %slice.203), channel_id=1, source_target_pairs={{2,0},{4,2},{6,4},{8,6},{10,8},{12,10},{14,12},{16,14},{18,16},{20... | collective-permute-start | bytes 98312 | tf_op jit(solution)/shard_map/ppermute | solution.py:16
Sparse Core Ops, SparseCore 0:
  22.8 17.3 reduce-scatter.4
  44.3 57.6 reduce-scatter.2
where the time goes:
time: 139 us; the launch traced here: 138 us
  between operations  64.6 us (46%)
  blocking collectives  37.2 us (27%)
  other arithmetic  12.2 us (9%)
  matrix products  10.6 us (8%)
  local copies, waits for them, and re-layouts  9.25 us (7%)
  starting transfers between devices  3.77 us (3%)
    psum x1, blocking collectives, per_device(): ar_grad = lax.psum(ar_part, 'tm')  37.2 us
    broadcast_in_dim x2, local copies, waits for them, and re-layouts, per_device(): keep = jnp.repeat(jnp.repeat(tile_mask, TILE, 0), TILE, 1) > 0  6.44 us
    reduce_sum x3, other arithmetic, per_device(): ar_rows.append(-scale_time * jnp.sum(error * behind, axis=0))  5.29 us
    dot_general x1, matrix products, per_device(): jnp.dot(residual, time_factors, preferred_element_type=jnp.float32)  4.42 us
    dot_general x1, matrix products, per_device(): jnp.dot(series_factors, time_factors.T, preferred_element_type=jnp.float32)  4.07 us
    ppermute x2, starting transfers between devices, from_behind(): lax.ppermute(value, axis, [(source, source + steps) for source in range(i...  3.69 us
    sub x1, other arithmetic, per_device(): adjoint = adjoint - ar_weights[lag_pos] * ahead  3.26 us
  transfers between devices with their start and end apart: 4, of which 0 were waited for; matrix products, arithmetic and copies ran while one was open for 12% of the time, Pallas kernels for 0%

commit v1 on v0

--- a/solution.py
+++ b/solution.py
@@ -64,7 +64,7 @@
         ar_rows.append(-scale_time * jnp.sum(error * behind, axis=0))
     ar_part = jnp.stack(ar_rows)
     series_grad = lax.psum_scatter(series_part, "tm", scatter_dimension=0, tiled=True)
-    ar_grad = lax.psum(ar_part, "tm")
+    ar_grad = jnp.sum(lax.all_gather(ar_part, "tm"), axis=0)
     time_share = lax.psum_scatter(time_part, "series", scatter_dimension=0, tiled=True)
     own_time = time_rows // series_devices
     adjoint_rows = lax.dynamic_slice_in_dim(

time: 139 us -> 128 us (0.921)
  blocking collectives: 37.2 us -> 25.5 us
    psum x1 -> x0, blocking collectives: 37.2 us -> none  [per_device(): ar_grad = lax.psum(ar_part, 'tm')]
    all_gather x0 -> x1, blocking collectives: none -> 25.5 us  [per_device(): ar_grad = jnp.sum(lax.all_gather(ar_part, 'tm'), axis=0)]
  transfers between devices with their start and end apart: 4 -> 4, of which waited for: 0 -> 0; matrix products, arithmetic and copies ran while one was open for 12% -> 14% of each run, Pallas kernels for 0% -> 0%
where the time goes in v1:
time: 128 us; the launch traced here: 127 us
  between operations  64.6 us (50%)
  blocking collectives  25.5 us (20%)
  other arithmetic  12.8 us (10%)
  matrix products  10.6 us (8%)
  local copies, waits for them, and re-layouts  9.25 us (7%)
  starting transfers between devices  3.77 us (3%)
    all_gather x1, blocking collectives, per_device(): ar_grad = jnp.sum(lax.all_gather(ar_part, 'tm'), axis=0)  25.5 us
    broadcast_in_dim x2, local copies, waits for them, and re-layouts, per_device(): keep = jnp.repeat(jnp.repeat(tile_mask, TILE, 0), TILE, 1) > 0  6.44 us
    reduce_sum x3, other arithmetic, per_device(): ar_rows.append(-scale_time * jnp.sum(error * behind, axis=0))  5.29 us
    dot_general x1, matrix products, per_device(): jnp.dot(residual, time_factors, preferred_element_type=jnp.float32)  4.42 us
    dot_general x1, matrix products, per_device(): jnp.dot(series_factors, time_factors.T, preferred_element_type=jnp.float32)  4.07 us
    ppermute x2, starting transfers between devices, from_behind(): lax.ppermute(value, axis, [(source, source + steps) for source in range(i...  3.69 us
    sub x1, other arithmetic, per_device(): adjoint = adjoint - ar_weights[lag_pos] * ahead  3.26 us
  transfers between devices with their start and end apart: 4, of which 0 were waited for; matrix products, arithmetic and copies ran while one was open for 14% of the time, Pallas kernels for 0%

profile of v1, /device:TPU:0, one launch (start us, length us, event | category | flops | bytes accessed | tf_op | source)
XLA Modules:
  0.0 126.5 jit_solution(11393759370098559169)
XLA Ops:
  7.2 0.0 reduce-scatter.5.cloned.1.call-start
  7.2 0.7 broadcast_compare_fusion
  8.0 0.1 copy.9
  8.1 0.1 broadcast_in_dim.23
  8.1 6.4 %broadcast_in_dim.24 = pred[2048,8,128]{2,1,0:T(8,128)(4,1)S(1)} broadcast(pred[2048,8]{1,0:T(8,128)(4,1)S(1)} %bitcast.92), dimensions={0,1} | broadcast | bytes 2113536 | tf_op jit(solution)/shard_map/broadcast_in_dim | solution.py:36
  14.5 4.1 %select_convert_fusion = bf16[2048,1024]{1,0:T(8,128)(2,1)S(1)} fusion(bf16[2048,1024]{1,0:T(8,128)(2,1)} %param.6, pred[256,8,8,128]{3,2,1,0:T(8,128)(4,1)S(1)} %bitcast.91, bf16[2048,128]{1,0:T(8,128)(2,1)S(1)} %copy-done, bf16[1024,128]{1,0:T(8,128)(2,1)} %param.8), kind=kOutput, calls=%fused_computation | convolution fusion | flops 545259520 | bytes 11272192 | tf_op jit(solution)/shard_map/dot_general | solution.py:37
  18.6 1.9 %copy-done.1 = bf16[2048,1024]{1,0:T(8,128)(2,1)} copy-done((bf16[2048,1024]{1,0:T(8,128)(2,1)}, bf16[2048,1024]{1,0:T(8,128)(2,1)S(1)}, u32[]{:S(2)}) %copy-start.1) | copy-done | bytes 4194328
  20.5 2.1 %convolution_multiply_fusion.1 = f32[1024,128]{1,0:T(8,128)} fusion(bf16[2048,1024]{1,0:T(8,128)(2,1)S(1)} %select_convert_fusion, bf16[2048,128]{1,0:T(8,128)(2,1)S(1)} %copy-done), kind=kOutput, calls=%fused_computation.34 | convolution fusion | flops 537001984 | bytes 5242880 | tf_op jit(solution)/shard_map/dot_general | solution.py:43
  22.6 0.0 reduce-scatter.3.cloned.1.call-start
  22.7 2.4 %collective-permute-start = (bf16[128,128]{1,0:T(8,128)(2,1)S(1)}, bf16[128,128]{1,0:T(8,128)(2,1)S(1)}, u32[]{:S(2)}, u32[]{:S(2)}) collective-permute-start(bf16[128,128]{1,0:T(8,128)(2,1)S(1)} %slice.70), channel_id=1, source_target_pairs={{0,2},{2,4},{4,6},{6,8},{8,10},{10,12},{12,14},{14,16},{16,18},{18... | collective-permute-start | bytes 98312 | tf_op jit(solution)/shard_map/ppermute | solution.py:16
  25.1 4.4 %convolution_multiply_fusion = f32[2048,128]{1,0:T(8,128)} fusion(bf16[2048,1024]{1,0:T(8,128)(2,1)} %copy-done.1, bf16[1024,128]{1,0:T(8,128)(2,1)S(1)} %copy-done.2), kind=kOutput, calls=%fused_computation.33 | convolution fusion | flops 537133056 | bytes 5505024 | tf_op jit(solution)/shard_map/dot_general | solution.py:41
  29.5 0.0 reduce-scatter.3.cloned.1.call-update
  29.6 0.7 fusion.63
  80.7 4.1 %multiply_reduce_fusion = (f32[128]{0:T(128)S(1)}, f32[128]{0:T(128)S(1)}, f32[128]{0:T(128)S(1)}, f32[128]{0:T(128)S(1)}, f32[128]{0:T(128)S(1)}, /*index=5*/f32[128]{0:T(128)S(1)}, f32[1024,128]{1,0:T(8,128)S(1)}) fusion(s32[]{:T(128)S(6)} %select_n.139, f32[1024,128]{1,0:T(8,128)S(1)} %convert_element_type.18, f32[128,128]{1,0:T(8,128)S(1)} %convert_element_type.19, ...), kind=kLoop, calls=%fused_computation.116 | loop fusion | flops 8912128 | bytes 1388608 | tf_op jit(solution)/shard_map/reduce_sum | solution.py:64
  84.8 0.5 multiply_reduce_fusion.12
  85.3 0.7 multiply_reduce_fusion.6
  86.0 1.3 %collective-permute-start.1 = (bf16[128,128]{1,0:T(8,128)(2,1)S(1)}, bf16[128,128]{1,0:T(8,128)(2,1)S(1)}, u32[]{:S(2)}, u32[]{:S(2)}) collective-permute-start(bf16[128,128]{1,0:T(8,128)(2,1)S(1)} %slice.203), channel_id=1, source_target_pairs={{2,0},{4,2},{6,4},{8,6},{10,8},{12,10},{14,12},{16,14},{18,16},{20... | collective-permute-start | bytes 98312 | tf_op jit(solution)/shard_map/ppermute | solution.py:16
  87.4 0.1 stack.2
  87.5 25.5 %all-gather = f32[256,128]{1,0:T(8,128)S(1)} all-gather(f32[16,128]{1,0:T(8,128)S(1)} %stack.2), channel_id=2, replica_groups=mesh['tm'=16,'series'=2] {'tm'}, dimensions={0}, use_global_device_ids=true | all-gather | bytes 139264 | tf_op jit(solution)/shard_map/all_gather | solution.py:67
  113.0 0.6 reduce_sum.169
  113.6 0.5 fusion.31
  114.2 3.3 %fusion.11 = f32[1024,128]{1,0:T(8,128)S(1)} fusion(f32[1024,128]{1,0:T(8,128)S(1)} %get-tuple-element.19, s32[]{:T(128)S(6)} %select_n.141, s32[]{:T(128)S(6)} %select_n.142, s32[]{:T(128)S(6)} %select_n.143, s32[]{:T(128)S(6)} %select_n.144, s32[]{:T(128)S(6)} %select_n.145, s32[]{:T(128)S(6)} %select_n.146, s32[]{:T(128)S(6)} %select_n.147, ...), kind=kLoop, calls=%fused_computation.78 | loop fusion | flops 3932160 | bytes 1119272 | tf_op jit(solution)/shard_map/sub | solution.py:62
  117.4 0.0 reduce-scatter.5.cloned.1.call-done
  117.4 2.2 %fusion.52 = f32[512,128]{1,0:T(8,128)} fusion(f32[512,128]{1,0:T(8,128)} %reduce-scatter.5.cloned.1.call-done, s32[]{:T(128)S(6)} %add.190, f32[1024,128]{1,0:T(8,128)S(1)} %get-tuple-element.19, s32[]{:T(128)S(6)} %add.184, s32[]{:T(128)S(6)} %add.186, s32[]{:T(128)S(6)} %add.188, f32[128,128]{1,0:T(8,128)S(1)} %convert_element_type.20, ...), kind=kLoop, calls=%fused_computation.136 | loop fusion | flops 1048576 | bytes 1903124 | tf_op jit(solution)/shard_map/add | solution.py:73
  (28 shorter events, 0.2 us)
Async XLA Ops:
  7.2 7.3 %copy-start = (bf16[2048,128]{1,0:T(8,128)(2,1)S(1)}, bf16[2048,128]{1,0:T(8,128)(2,1)}, u32[]{:S(2)}) copy-start(bf16[2048,128]{1,0:T(8,128)(2,1)} %param.7) | copy-start | bytes 1572868
  7.2 110.3 %reduce-scatter.5.cloned.1.call-start = ((), (), s32[]{:S(2)}) async-start(), calls=%async_computation.3 | async-start | bytes 786432 | tf_op jit(solution)/shard_map/reduce_scatter | solution.py:68
  18.6 1.9 %copy-start.1 = (bf16[2048,1024]{1,0:T(8,128)(2,1)}, bf16[2048,1024]{1,0:T(8,128)(2,1)S(1)}, u32[]{:S(2)}) copy-start(bf16[2048,1024]{1,0:T(8,128)(2,1)S(1)} %select_convert_fusion) | copy-start | bytes 12582916
  20.5 2.2 %copy-start.2 = (bf16[1024,128]{1,0:T(8,128)(2,1)S(1)}, bf16[1024,128]{1,0:T(8,128)(2,1)}, u32[]{:S(2)}) copy-start(bf16[1024,128]{1,0:T(8,128)(2,1)} %param.8) | copy-start | bytes 786436
  22.6 7.0 %copy-start.3 = (s32[16]{0:T(128)S(1)}, s32[16]{0:T(128)}, u32[]{:S(2)}) copy-start(s32[16]{0:T(128)} %param.11) | copy-start | bytes 196
  22.6 7.7 %copy-start.4 = (f32[16,128]{1,0:T(8,128)S(1)}, f32[16,128]{1,0:T(8,128)}, u32[]{:S(2)}) copy-start(f32[16,128]{1,0:T(8,128)} %param.9) | copy-start | bytes 24580
  22.6 97.0 %reduce-scatter.3.cloned.1.call-start = ((), (), s32[]{:S(2)}) async-start(), calls=%async_computation.2 | async-start | bytes 1114112 | tf_op jit(solution)/shard_map/reduce_scatter | solution.py:66
  22.7 58.0 %collective-permute-start = (bf16[128,128]{1,0:T(8,128)(2,1)S(1)}, bf16[128,128]{1,0:T(8,128)(2,1)S(1)}, u32[]{:S(2)}, u32[]{:S(2)}) collective-permute-start(bf16[128,128]{1,0:T(8,128)(2,1)S(1)} %slice.70), channel_id=1, source_target_pairs={{0,2},{2,4},{4,6},{6,8},{8,10},{10,12},{12,14},{14,16},{16,18},{18... | collective-permute-start | bytes 98312 | tf_op jit(solution)/shard_map/ppermute | solution.py:16
  86.0 27.6 %collective-permute-start.1 = (bf16[128,128]{1,0:T(8,128)(2,1)S(1)}, bf16[128,128]{1,0:T(8,128)(2,1)S(1)}, u32[]{:S(2)}, u32[]{:S(2)}) collective-permute-start(bf16[128,128]{1,0:T(8,128)(2,1)S(1)} %slice.203), channel_id=1, source_target_pairs={{2,0},{4,2},{6,4},{8,6},{10,8},{12,10},{14,12},{16,14},{18,16},{20... | collective-permute-start | bytes 98312 | tf_op jit(solution)/shard_map/ppermute | solution.py:16
Sparse Core Ops, SparseCore 0:
  22.8 17.3 reduce-scatter.4
  44.3 57.6 reduce-scatter.2
